TPU v7x, 32 devices: a whole 2x2x4 slice. The times are simulated.
32 devices in a mesh: grp: 2 (over x), tm: 16 (over z, y, core).
Axes of the slice: x: 2, y: 2, z: 4, core: 2. Of those that a mesh axis runs over, the one named last changes fastest.
Arguments:
- block_input: bfloat16 [4, 16, 120, 384], P('grp', 'tm'), parts along dimension 0, may hold values from -6 to 6
- hidden_state: bfloat16 [4, 16, 120, 384], P('grp', 'tm'), parts along dimension 0, may hold values from -6 to 6
- norm_gain: float32 [384], replicated, may hold values from 0.5 to 1.5
- conv_weight: bfloat16 [3, 3, 3, 384, 384], replicated, may hold values from -0.0625 to 0.0625
- attn_gain: float32 [384], replicated, may hold values from 0.5 to 1.5
- qkv_weight: bfloat16 [384, 1152], replicated, may hold values from -4 to 4
- proj_weight: bfloat16 [384, 384], replicated, may hold values from -0.3125 to 0.3125
Outputs:
- block_output: bfloat16 [4, 16, 120, 384], P('grp', 'tm'), parts along dimension 0
There are 2 independent parts, one for each index of `grp`. A program takes and returns all parts, laid end to end along the dimension named above; an argument that names none is the same for every part. Nothing has to cross between parts.
All inputs are finite; a program needn't handle non-finite values.
Results may differ from a plain program's by a relative error of at most 0.006.
Values may be sent and summed in bfloat16 or wider, within the bound.
A program may use at most 128 MiB of HBM per device.

v0:
```python
import jax
import jax.numpy as jnp
from jax import lax
from jax.sharding import PartitionSpec as P


def with_halo(x, sides, width):
    for axis, dim in sides:
        peers, length = (lax.axis_size(axis), x.shape[dim])
        up = [(i, (i + 1) % peers) for i in range(peers - 1)]
        down = [(j, i) for i, j in up]
        last = lax.slice_in_dim(x, length - width, length, axis=dim)
        leading = lax.slice_in_dim(x, 0, width, axis=dim)
        before = lax.ppermute(last, axis, up)
        after = lax.ppermute(leading, axis, down)
        x = jnp.concatenate([before, x, after], axis=dim)
    return x


def rms_scale(values, gain):
    wide = values.astype(jnp.float32)
    return wide * lax.rsqrt(jnp.mean(wide * wide, axis=-1, keepdims=True) + 1e-06) * gain


def causal_conv(padded, kernel):
    channels = padded.shape[-1]
    frames = padded.shape[0] - 2
    row_count = padded.shape[1] - 2
    col_count = padded.shape[2] - 2
    pieces = [
        padded[t_off : t_off + frames, r_off : r_off + row_count, c_off : c_off + col_count, :]
        for t_off in range(3)
        for r_off in range(3)
        for c_off in range(3)
    ]
    stacked = jnp.concatenate(pieces, axis=-1).reshape(-1, 27 * channels)
    result = jnp.dot(
        stacked, kernel.reshape(27 * channels, channels), preferred_element_type=jnp.float32
    )
    return result.reshape(frames, row_count, col_count, channels)


def attend(queries, key_value, mixed_frame, proj_weight):
    channels = queries.shape[-1]
    key_part = key_value[:, :channels]
    value_part = key_value[:, channels:]
    scores = jnp.dot(queries, key_part.T, preferred_element_type=jnp.float32) * channels ** (-0.5)
    scores = scores - jnp.max(scores, axis=-1, keepdims=True)
    expo = jnp.exp(scores)
    weights = (expo / jnp.sum(expo, axis=-1, keepdims=True)).astype(jnp.bfloat16)
    attended = jnp.dot(weights, value_part, preferred_element_type=jnp.float32).astype(jnp.bfloat16)
    result = mixed_frame.reshape(-1, channels).astype(jnp.float32) + jnp.dot(
        attended, proj_weight, preferred_element_type=jnp.float32
    )
    return result.astype(jnp.bfloat16).reshape(mixed_frame.shape)


def body(block_input, hidden_state, norm_gain, conv_weight, attn_gain, qkv_weight, proj_weight):
    channels = block_input.shape[-1]
    frames = block_input.shape[0]
    conv_in = jax.nn.silu(rms_scale(hidden_state, norm_gain)).astype(jnp.bfloat16)
    padded = with_halo(conv_in, (("tm", 1),), 1)
    padded = jnp.pad(padded, ((2, 0), (0, 0), (1, 1), (0, 0)))
    conv_out = causal_conv(padded, conv_weight)
    mixed = (block_input.astype(jnp.float32) + conv_out).astype(jnp.bfloat16)
    normed = rms_scale(mixed, attn_gain).astype(jnp.bfloat16)
    local_rows = normed.shape[1] * normed.shape[2]
    projected = jnp.dot(
        normed.reshape(-1, channels), qkv_weight, preferred_element_type=jnp.float32
    ).astype(jnp.bfloat16)
    queries = projected[:, :channels].reshape(frames, local_rows, channels)
    key_value = projected[:, channels:].reshape(
        frames, normed.shape[1], normed.shape[2], 2 * channels
    )
    whole = lax.all_gather(key_value, "tm", axis=1, tiled=True)
    whole = whole.reshape(frames, -1, 2 * channels)
    return lax.map(
        lambda triple: attend(triple[0], triple[1], triple[2], proj_weight), (queries, whole, mixed)
    )


def solution(mesh):
    return jax.shard_map(
        body,
        mesh=mesh,
        in_specs=(P("grp", "tm", None, None), P("grp", "tm", None, None), P(), P(), P(), P(), P()),
        out_specs=P("grp", "tm", None, None),
        check_vma=False,
    )
```

profile of v0, /device:TPU:0, one launch (start us, length us, event | category | flops | bytes accessed | tf_op | source)
XLA Modules:
  0.0 113.6 jit_solution(8456333361618802162)
XLA Ops:
  6.5 1.1 fusion.44
  7.7 1.1 fusion.51
  8.8 1.6 %collective-permute-start.1 = (bf16[2,1,120,384]{3,2,0,1:T(8,128)(2,1)S(1)}, bf16[2,1,120,384]{3,2,0,1:T(8,128)(2,1)S(1)}, u32[]{:S(2)}, u32[]{:S(2)}) collective-permute-start(bf16[2,1,120,384]{3,2,0,1:T(8,128)(2,1)S(1)} %fusion.51), channel_id=1, source_target_pairs={{1,0},{2,1},{3,2},{4,3},{5,4},{6,5},{7,6},{8,7},{9,8},{10,9},{11,1... | collective-permute-start | bytes 552968 | tf_op jit(solution)/shard_map/ppermute | solution.py:15
  10.4 3.2 %collective-permute-start = (bf16[2,1,120,384]{3,2,0,1:T(8,128)(2,1)S(1)}, bf16[2,1,120,384]{3,2,0,1:T(8,128)(2,1)S(1)}, u32[]{:S(2)}, u32[]{:S(2)}) collective-permute-start(bf16[2,1,120,384]{3,2,0,1:T(8,128)(2,1)S(1)} %fusion.51), channel_id=1, source_target_pairs={{0,1},{1,2},{2,3},{3,4},{4,5},{5,6},{6,7},{7,8},{8,9},{9,10},{10,1... | collective-permute-start | bytes 552968 | tf_op jit(solution)/shard_map/ppermute | solution.py:14
  13.9 0.7 collective-permute-done
  14.6 0.2 fusion.35
  14.8 0.1 slice_dynamic-update-slice_fusion.13
  14.9 0.1 slice_dynamic-update-slice_fusion.12
  15.0 0.1 slice_dynamic-update-slice_fusion.10
  15.1 0.1 slice_dynamic-update-slice_fusion.9
  15.2 0.1 slice_dynamic-update-slice_fusion.7
  15.2 0.1 slice_dynamic-update-slice_fusion.6
  15.5 0.2 constant_dynamic-update-slice_fusion.1
  15.7 0.1 slice_dynamic-update-slice_fusion.2
  16.0 3.0 %fusion.52 = (f32[2,120]{1,0:T(2,128)S(1)}, bf16[2,1,120,384]{3,2,0,1:T(8,128)(2,1)S(1)}) fusion(bf16[10368,384,1]{1,0,2:T(8,128)(2,1)S(1)} %bitcast.67, bf16[2,1,120,10368]{3,2,0,1:T(8,128)(2,1)S(1)} %slice_dynamic-update-slice_fusion, bf16[2,1,120,384]{3,2,1,0:T(8,128)(2,1)S(1)} %copy-done.8), kind=kOutput, calls=%fused_computation.49 | convolution fusion | flops 1911582464 | bytes 13308864 | tf_op jit(solution)/shard_map/dot_general | solution.py:37
  19.0 0.1 fusion.54
  19.1 0.5 convolution_convert_fusion
  19.6 0.8 slice.107
  20.4 66.2 %all-gather.2.cloned.1.call-done = bf16[2,16,120,768]{3,2,0,1:T(8,128)(2,1)} async-done(((bf16[2,1,120,768]{3,2,0,1:T(8,128)(2,1)}), bf16[2,16,120,768]{3,2,0,1:T(8,128)(2,1)}) %all-gather.2.cloned.1.call-update) | async-done | bytes 5898256 | tf_op jit(solution)/shard_map/all_gather | solution.py:75
  86.6 5.6 %copy.19 = bf16[2,16,120,768]{3,2,1,0:T(8,128)(2,1)} copy(bf16[2,16,120,768]{3,2,0,1:T(8,128)(2,1)} %all-gather.2.cloned.1.call-done) | data formatting | bytes 11796480 | tf_op jit(solution)/shard_map/all_gather | solution.py:75
  92.2 13.8 %while.10 = (s32[]{:T(128)}, bf16[2,1,120,384]{3,2,1,0:T(8,128)(2,1)S(1)}, bf16[2,1,120,384]{3,2,1,0:T(8,128)(2,1)S(1)}, bf16[2,120,384]{2,1,0:T(8,128)(2,1)S(1)...) while((s32[]{:T(128)}, bf16[2,1,120,384]{3,2,1,0:T(8,128)(2,1)S(1)}, ...), condition=%wide.region_5.6_spmd, body=%wide.region_2.5_spmd.sunk | while | flops 391080704 | bytes 23982620 | solution.py:77
  92.2 2.0 %dynamic-slice_bitcast_fusion.2 = bf16[1920,768]{1,0:T(8,128)(2,1)S(1)} fusion(bf16[2,1920,768]{2,1,0:T(8,128)(2,1)} %get-tuple-element.131, s32[]{:T(128)S(6)} %copy.51), kind=kLoop, calls=%fused_computation.clone.1 | loop fusion | bytes 5898244 | tf_op jit(solution)/shard_map/while/body/jit(dynamic_index_in_dim)/squeeze | solution.py:77
  94.2 1.6 %copy-done.1 = bf16[1920,768]{1,0:T(8,128)(2,1)} copy-done((bf16[1920,768]{1,0:T(8,128)(2,1)}, bf16[1920,768]{1,0:T(8,128)(2,1)S(1)}, u32[]{:S(2)}) %copy-start.1) | copy-done | bytes 2949144 | tf_op jit(solution)/shard_map/while
  95.9 0.9 fusion.67
  96.7 0.3 fusion.68
  97.0 2.1 %fusion.69 = bf16[2,1,120,384]{3,2,1,0:T(8,128)(2,1)S(1)} fusion(bf16[2,1,120,384]{3,2,1,0:T(8,128)(2,1)S(1)} %get-tuple-element.121, s32[]{:T(128)S(6)} %copy.51, bf16[384,384]{1,0:T(8,128)(2,1)S(1)} %get-tuple-element.132, bf16[1920,768]{1,0:T(8,128)(2,1)} %copy-done.1, f32[120,1920]{1,0:T(8,128)S(1)} %get-tuple-element.111, f32[120]{0:T(128)S(1)} %fusion.68, ...), kind=kOutput, calls=%fused_computation.9.clone.1 | convolution fusion | flops 213212160 | bytes 2876420 | tf_op jit(solution)/shard_map/while/body/eval_jaxpr/dot_general | solution.py:52
  99.1 2.0 %dynamic-slice_bitcast_fusion.2 = bf16[1920,768]{1,0:T(8,128)(2,1)S(1)} fusion(bf16[2,1920,768]{2,1,0:T(8,128)(2,1)} %get-tuple-element.131, s32[]{:T(128)S(6)} %copy.51), kind=kLoop, calls=%fused_computation.clone.1 | loop fusion | bytes 5898244 | tf_op jit(solution)/shard_map/while/body/jit(dynamic_index_in_dim)/squeeze | solution.py:77
  101.2 1.6 %copy-done.1 = bf16[1920,768]{1,0:T(8,128)(2,1)} copy-done((bf16[1920,768]{1,0:T(8,128)(2,1)}, bf16[1920,768]{1,0:T(8,128)(2,1)S(1)}, u32[]{:S(2)}) %copy-start.1) | copy-done | bytes 2949144 | tf_op jit(solution)/shard_map/while
  102.8 0.9 fusion.67
  103.7 0.3 fusion.68
  104.0 2.1 %fusion.69 = bf16[2,1,120,384]{3,2,1,0:T(8,128)(2,1)S(1)} fusion(bf16[2,1,120,384]{3,2,1,0:T(8,128)(2,1)S(1)} %get-tuple-element.121, s32[]{:T(128)S(6)} %copy.51, bf16[384,384]{1,0:T(8,128)(2,1)S(1)} %get-tuple-element.132, bf16[1920,768]{1,0:T(8,128)(2,1)} %copy-done.1, f32[120,1920]{1,0:T(8,128)S(1)} %get-tuple-element.111, f32[120]{0:T(128)S(1)} %fusion.68, ...), kind=kOutput, calls=%fused_computation.9.clone.1 | convolution fusion | flops 213212160 | bytes 2876420 | tf_op jit(solution)/shard_map/while/body/eval_jaxpr/dot_general | solution.py:52
  106.1 0.7 copy-done.3
  (43 shorter events, 0.8 us)
Async XLA Ops:
  6.5 12.6 %copy-start = (bf16[384,1152]{1,0:T(8,128)(2,1)S(1)}, bf16[384,1152]{1,0:T(8,128)(2,1)}, u32[]{:S(2)}) copy-start(bf16[384,1152]{1,0:T(8,128)(2,1)} %param.14) | copy-start | bytes 2654212
  6.5 9.0 %copy-start.2 = (bf16[2,1,120,384]{3,2,1,0:T(8,128)(2,1)S(1)}, bf16[2,1,120,384]{3,2,1,0:T(8,128)(2,1)}, u32[]{:S(2)}) copy-start(bf16[2,1,120,384]{3,2,1,0:T(8,128)(2,1)} %param.10) | copy-start | bytes 552964
  6.5 9.0 %copy-start.4 = (f32[384]{0:T(512)S(1)}, f32[384]{0:T(512)}, u32[]{:S(2)}) copy-start(f32[384]{0:T(512)} %param.11) | copy-start | bytes 4612
  6.5 80.1 %all-gather.2.cloned.1.call-start = ((), (), s32[]{:S(2)}) async-start(), calls=%async_computation | async-start | bytes 6266880 | tf_op jit(solution)/shard_map/all_gather | solution.py:75
  8.8 7.1 %copy-start.6 = (bf16[3,3,3,384,384]{4,3,2,1,0:T(8,128)(2,1)S(1)}, bf16[3,3,3,384,384]{4,3,2,1,0:T(8,128)(2,1)}, u32[]{:S(2)}) copy-start(bf16[3,3,3,384,384]{4,3,2,1,0:T(8,128)(2,1)} %param.12) | copy-start | bytes 23887876
  8.8 7.1 %copy-start.8 = (bf16[2,1,120,384]{3,2,1,0:T(8,128)(2,1)S(1)}, bf16[2,1,120,384]{3,2,1,0:T(8,128)(2,1)}, u32[]{:S(2)}) copy-start(bf16[2,1,120,384]{3,2,1,0:T(8,128)(2,1)} %param.9) | copy-start | bytes 552964
  8.8 5.0 %collective-permute-start.1 = (bf16[2,1,120,384]{3,2,0,1:T(8,128)(2,1)S(1)}, bf16[2,1,120,384]{3,2,0,1:T(8,128)(2,1)S(1)}, u32[]{:S(2)}, u32[]{:S(2)}) collective-permute-start(bf16[2,1,120,384]{3,2,0,1:T(8,128)(2,1)S(1)} %fusion.51), channel_id=1, source_target_pairs={{1,0},{2,1},{3,2},{4,3},{5,4},{6,5},{7,6},{8,7},{9,8},{10,9},{11,1... | collective-permute-start | bytes 552968 | tf_op jit(solution)/shard_map/ppermute | solution.py:15
  10.4 4.2 %collective-permute-start = (bf16[2,1,120,384]{3,2,0,1:T(8,128)(2,1)S(1)}, bf16[2,1,120,384]{3,2,0,1:T(8,128)(2,1)S(1)}, u32[]{:S(2)}, u32[]{:S(2)}) collective-permute-start(bf16[2,1,120,384]{3,2,0,1:T(8,128)(2,1)S(1)} %fusion.51), channel_id=1, source_target_pairs={{0,1},{1,2},{2,3},{3,4},{4,5},{5,6},{6,7},{7,8},{8,9},{9,10},{10,1... | collective-permute-start | bytes 552968 | tf_op jit(solution)/shard_map/ppermute | solution.py:14
  15.9 3.0 %copy-start.5 = (f32[384]{0:T(512)S(1)}, f32[384]{0:T(512)}, u32[]{:S(2)}) copy-start(f32[384]{0:T(512)} %param.13) | copy-start | bytes 4612
  20.4 71.8 %copy-start.7 = (bf16[384,384]{1,0:T(8,128)(2,1)S(1)}, bf16[384,384]{1,0:T(8,128)(2,1)}, u32[]{:S(2)}) copy-start(bf16[384,384]{1,0:T(8,128)(2,1)} %param.15) | copy-start | bytes 884740
  94.2 1.7 %copy-start.1 = (bf16[1920,768]{1,0:T(8,128)(2,1)}, bf16[1920,768]{1,0:T(8,128)(2,1)S(1)}, u32[]{:S(2)}) copy-start(bf16[1920,768]{1,0:T(8,128)(2,1)S(1)} %dynamic-slice_bitcast_fusion.2) | copy-start | bytes 8847364 | tf_op jit(solution)/shard_map/while
  101.1 1.7 %copy-start.1 = (bf16[1920,768]{1,0:T(8,128)(2,1)}, bf16[1920,768]{1,0:T(8,128)(2,1)S(1)}, u32[]{:S(2)}) copy-start(bf16[1920,768]{1,0:T(8,128)(2,1)S(1)} %dynamic-slice_bitcast_fusion.2) | copy-start | bytes 8847364 | tf_op jit(solution)/shard_map/while
  106.0 0.7 copy-start.3
Sparse Core Ops, SparseCore 0:
  20.5 66.0 all-gather.1
where the time goes:
time: 114 us
  waiting for transfers between devices  66.9 us (59%)
  local copies, waits for them, and re-layouts  15.5 us (14%)
  between operations  13.7 us (12%)
  matrix products  9.36 us (8%)
  starting transfers between devices  4.73 us (4%)
  other arithmetic  3.35 us (3%)
    all_gather x1, waiting for transfers between devices, body(): whole = lax.all_gather(key_value, 'tm', axis=1, tiled=True)  66.2 us
    all_gather x1, local copies, waits for them, and re-layouts, body(): whole = lax.all_gather(key_value, 'tm', axis=1, tiled=True)  5.57 us
    dot_general x2, matrix products, attend(): jnp.dot(attended, proj_weight, preferred_element_type=jnp.float32)  4.14 us
    squeeze x2, local copies, waits for them, and re-layouts, body(): lax.map(lambda triple: attend(triple[0], triple[1], triple[2], proj_weigh...  4.05 us
    while x4, local copies, waits for them, and re-layouts  3.29 us
    ppermute x1, starting transfers between devices, with_halo(): before = lax.ppermute(last, axis, up)  3.17 us
    dot_general x1, matrix products, causal_conv(): jnp.dot(stacked, kernel.reshape(27 * channels, channels), preferred_eleme...  2.99 us
  transfers between devices with their start and end apart: 3, of which 2 were waited for; matrix products, arithmetic and copies ran while one was open for 0% of the time, Pallas kernels for 0%

commit v1 on v0

v1 whole, which is shorter than its diff:
```python
import functools

import jax
import jax.numpy as jnp
from jax import lax
from jax.experimental import pallas as pl
from jax.experimental.pallas import tpu as pltpu
from jax.sharding import PartitionSpec as P

CORES = 2


def halo_kernel(n, x_ref, before_ref, after_ref, sems, recv):
    me = lax.axis_index("tm")
    rows = x_ref.shape[1]
    barrier = pltpu.get_barrier_semaphore()

    @pl.when(me > 0)
    def _():
        pl.semaphore_signal(barrier, inc=1, device_id={"tm": me - 1})

    @pl.when(me < n - 1)
    def _():
        pl.semaphore_signal(barrier, inc=1, device_id={"tm": me + 1})

    inner = jnp.logical_and(me > 0, me < n - 1)
    pl.semaphore_wait(barrier, jnp.where(inner, 2, 1))

    def to_next():
        return pltpu.make_async_remote_copy(
            x_ref.at[:, rows - 1], before_ref, sems.at[0], recv.at[0], device_id={"tm": me + 1}
        )

    def to_previous():
        return pltpu.make_async_remote_copy(
            x_ref.at[:, 0], after_ref, sems.at[1], recv.at[1], device_id={"tm": me - 1}
        )

    @pl.when(me < n - 1)
    def _():
        to_next().start()

    @pl.when(me > 0)
    def _():
        to_previous().start()

    @pl.when(me == 0)
    def _():
        before_ref[...] = jnp.zeros_like(before_ref)

    @pl.when(me == n - 1)
    def _():
        after_ref[...] = jnp.zeros_like(after_ref)

    @pl.when(me < n - 1)
    def _():
        to_next().wait_send()
        to_previous().wait_recv()

    @pl.when(me > 0)
    def _():
        to_previous().wait_send()
        to_next().wait_recv()


def halo(x, n):
    frames, _, cols, channels = x.shape
    edge = jax.ShapeDtypeStruct((frames, cols, channels), x.dtype)
    vmem = pl.BlockSpec(memory_space=pltpu.VMEM)
    return pl.pallas_call(
        functools.partial(halo_kernel, n),
        out_shape=(edge, edge),
        in_specs=[vmem],
        out_specs=(vmem, vmem),
        scratch_shapes=[pltpu.SemaphoreType.DMA((2,)), pltpu.SemaphoreType.DMA((2,))],
        compiler_params=pltpu.CompilerParams(collective_id=0, has_side_effects=True),
    )(x)


def gather_kernel(zn, yn, x_ref, out_ref, local_sem, up, down, across, twin, recv):
    frames = x_ref.shape[0]
    me = lax.axis_index("tm")
    c = lax.rem(me, CORES)
    y = lax.rem(me // CORES, yn)
    z = me // (CORES * yn)

    def index(zz, yy, cc):
        return (zz * yn + yy) * CORES + cc

    below, above = index(z - 1, y, c), index(z + 1, y, c)
    sibling, opposite = index(z, y, 1 - c), index(z, yn - 1 - y, c)
    has_below, has_above = z > 0, z < zn - 1

    barrier = pltpu.get_barrier_semaphore()
    pl.semaphore_signal(barrier, inc=1, device_id={"tm": sibling})
    if yn > 1:
        pl.semaphore_signal(barrier, inc=1, device_id={"tm": opposite})

    @pl.when(has_below)
    def _():
        pl.semaphore_signal(barrier, inc=1, device_id={"tm": below})

    @pl.when(has_above)
    def _():
        pl.semaphore_signal(barrier, inc=1, device_id={"tm": above})

    inner = jnp.logical_and(has_below, has_above)
    pl.semaphore_wait(barrier, yn + (jnp.where(inner, 2, 1) if zn > 1 else 0))

    def copy(zz, yy, cc, f, send, target, own=False):
        owner = index(zz, yy, cc)
        return pltpu.make_async_remote_copy(
            x_ref.at[f] if own else out_ref.at[f, owner],
            out_ref.at[f, owner],
            send,
            recv.at[owner, f],
            device_id={"tm": target},
        )

    def up_copy(zz, f, own=False):
        return copy(zz, y, c, f, up.at[zz, f], above, own)

    def down_copy(zz, f, own=False):
        return copy(zz, y, c, f, down.at[zz, f], below, own)

    def across_copy(zz, f, own=False):
        return copy(zz, y, c, f, across.at[zz, f], opposite, own)

    def twin_copy(zz, yy, f, own=False):
        return copy(zz, yy, c, f, twin.at[zz, yy, f], sibling, own)

    def arrived(zz, yy, cc, f):
        copy(zz, yy, cc, f, up.at[0, 0], sibling).wait_recv()

    def own_copy(f):
        return pltpu.make_async_copy(x_ref.at[f], out_ref.at[f, me], local_sem.at[f])

    for f in range(frames):

        @pl.when(has_above)
        def _():
            up_copy(z, f, True).start()

        @pl.when(has_below)
        def _():
            down_copy(z, f, True).start()

        if yn > 1:
            across_copy(z, f, True).start()
        twin_copy(z, y, f, True).start()
        own_copy(f).start()

    def from_across(zz, f):
        arrived(zz, yn - 1 - y, c, f)
        twin_copy(zz, yn - 1 - y, f).start()

    def step(d, part):
        for f in range(frames):

            @pl.when(z - d >= 0)
            def _():
                part(z - d, f, True)

            @pl.when(z + d < zn)
            def _():
                part(z + d, f, False)

    def along(zz, f, from_below):
        arrived(zz, y, c, f)
        if from_below:

            @pl.when(has_above)
            def _():
                up_copy(zz, f).start()
        else:

            @pl.when(has_below)
            def _():
                down_copy(zz, f).start()

        if yn > 1:
            across_copy(zz, f).start()
        twin_copy(zz, y, f).start()

    def crossed(zz, f, from_below):
        from_across(zz, f)

    for d in range(1, zn):
        step(d, along)
        if yn > 1:
            if d == 1:
                for f in range(frames):
                    from_across(z, f)
            else:
                step(d - 1, crossed)
    if yn > 1:
        if zn == 1:
            for f in range(frames):
                from_across(z, f)
        else:
            step(zn - 1, crossed)

    for zz in range(zn):
        for f in range(frames):
            for yy in range(yn):
                arrived(zz, yy, 1 - c, f)
                twin_copy(zz, yy, f).wait_send()
            if yn > 1:
                across_copy(zz, f).wait_send()

            @pl.when(jnp.logical_and(has_above, zz <= z))
            def _():
                up_copy(zz, f).wait_send()

            @pl.when(jnp.logical_and(has_below, zz >= z))
            def _():
                down_copy(zz, f).wait_send()

    for f in range(frames):
        own_copy(f).wait()


def gather(x, n):
    frames, rows, channels = x.shape
    yn = 2 if n % (2 * CORES) == 0 else 1
    zn = n // (CORES * yn)
    vmem = pl.BlockSpec(memory_space=pltpu.VMEM)
    dma = pltpu.SemaphoreType.DMA
    return pl.pallas_call(
        functools.partial(gather_kernel, zn, yn),
        out_shape=jax.ShapeDtypeStruct((frames, n, rows, channels), x.dtype),
        in_specs=[vmem],
        out_specs=vmem,
        scratch_shapes=[
            dma((frames,)),
            dma((zn, frames)),
            dma((zn, frames)),
            dma((zn, frames)),
            dma((zn, yn, frames)),
            dma((n, frames)),
        ],
        compiler_params=pltpu.CompilerParams(
            collective_id=1, has_side_effects=True, vmem_limit_bytes=48 * 2**20
        ),
    )(x)


def rms_scale(values, gain):
    wide = values.astype(jnp.float32)
    return wide * lax.rsqrt(jnp.mean(wide * wide, axis=-1, keepdims=True) + 1e-06) * gain


def causal_conv(padded, kernel):
    channels = padded.shape[-1]
    frames = padded.shape[0] - 2
    row_count = padded.shape[1] - 2
    col_count = padded.shape[2] - 2
    pieces = [
        padded[t_off : t_off + frames, r_off : r_off + row_count, c_off : c_off + col_count, :]
        for t_off in range(3)
        for r_off in range(3)
        for c_off in range(3)
    ]
    stacked = jnp.concatenate(pieces, axis=-1).reshape(-1, 27 * channels)
    result = jnp.dot(
        stacked, kernel.reshape(27 * channels, channels), preferred_element_type=jnp.float32
    )
    return result.reshape(frames, row_count, col_count, channels)


def attend(queries, normed, mixed_frame, qkv_weight, proj_weight):
    channels = queries.shape[-1]
    key_value = jnp.dot(
        normed, qkv_weight[:, channels:], preferred_element_type=jnp.float32
    ).astype(jnp.bfloat16)
    key_part = key_value[:, :channels]
    value_part = key_value[:, channels:]
    scores = jnp.dot(queries, key_part.T, preferred_element_type=jnp.float32) * channels ** (-0.5)
    scores = scores - jnp.max(scores, axis=-1, keepdims=True)
    expo = jnp.exp(scores)
    weights = (expo / jnp.sum(expo, axis=-1, keepdims=True)).astype(jnp.bfloat16)
    attended = jnp.dot(weights, value_part, preferred_element_type=jnp.float32).astype(jnp.bfloat16)
    result = mixed_frame.astype(jnp.float32) + jnp.dot(
        attended, proj_weight, preferred_element_type=jnp.float32
    )
    return result.astype(jnp.bfloat16)


def body(block_input, hidden_state, norm_gain, conv_weight, attn_gain, qkv_weight, proj_weight):
    n = lax.axis_size("tm")
    me = lax.axis_index("tm")
    frames, rows, cols, channels = block_input.shape
    before, after = halo(hidden_state, n)
    padded = jnp.concatenate([before[:, None], hidden_state, after[:, None]], axis=1)
    conv_in = jax.nn.silu(rms_scale(padded, norm_gain)).astype(jnp.bfloat16)
    padded = jnp.pad(conv_in, ((2, 0), (0, 0), (1, 1), (0, 0)))
    conv_out = causal_conv(padded, conv_weight)
    mixed = (block_input.astype(jnp.float32) + conv_out).astype(jnp.bfloat16)
    normed = rms_scale(mixed, attn_gain).astype(jnp.bfloat16)
    local = rows * cols
    normed = normed.reshape(frames, local, channels)
    mixed = mixed.reshape(frames, local, channels)
    queries = jnp.dot(
        normed, qkv_weight[:, :channels], preferred_element_type=jnp.float32
    ).astype(jnp.bfloat16)
    whole = gather(normed, n).reshape(frames, n * local, channels)
    outs = [
        attend(queries[f], whole[f], mixed[f], qkv_weight, proj_weight) for f in range(frames)
    ]
    return jnp.stack(outs).reshape(block_input.shape)


def solution(mesh):
    return jax.shard_map(
        body,
        mesh=mesh,
        in_specs=(P("grp", "tm", None, None), P("grp", "tm", None, None), P(), P(), P(), P(), P()),
        out_specs=P("grp", "tm", None, None),
        check_vma=False,
    )
```

time: 114 us -> 55.5 us (0.49)
  waiting for transfers between devices: 66.9 us -> 0 us
  Pallas kernels: 0 us -> 31.8 us
  between operations: 13.7 us -> 0.26 us
  local copies, waits for them, and re-layouts: 15.5 us -> 5.16 us
  starting transfers between devices: 4.73 us -> 0 us
  matrix products: 9.36 us -> 13.6 us
    all_gather x1 -> x0, waiting for transfers between devices: 66.2 us -> none  [body(): whole = lax.all_gather(key_value, 'tm', axis=1, tiled=True)]
    pallas_call x0 -> x2, Pallas kernels: none -> 31.8 us  [the longest x1 26.1 us: gather(): pl.pallas_call(functools.partial(gather_kernel, zn, yn), out_shape=jax.Sh...]
    all_gather x1 -> x0, local copies, waits for them, and re-layouts: 5.57 us -> none  [body(): whole = lax.all_gather(key_value, 'tm', axis=1, tiled=True)]
    ppermute x2 -> x0, starting transfers between devices: 4.73 us -> none  [the longest x1 3.17 us: with_halo(): before = lax.ppermute(last, axis, up)]
    dot_general x1 -> x3, matrix products: 0.48 us -> 4.75 us  [the longest x2 4.47 us: attend(): jnp.dot(normed, qkv_weight[:, channels:], preferred_element_type=jnp.floa...]
    squeeze x2 -> x0, local copies, waits for them, and re-layouts: 4.05 us -> none  [body(): lax.map(lambda triple: attend(triple[0], triple[1], triple[2], proj_weigh...]
    while x5 -> x0, local copies, waits for them, and re-layouts: 3.31 us -> none
    unnamed x41 -> x42, local copies, waits for them, and re-layouts: 1.72 us -> 4.8 us
  transfers between devices with their start and end apart: 3 -> 0, of which waited for: 2 -> 0; matrix products, arithmetic and copies ran while one was open for 0% -> 0% of each run, Pallas kernels for 0% -> 0%
where the time goes in v1:
time: 55.5 us; the launch traced here: 55.2 us
  Pallas kernels  31.8 us (57%)
  matrix products  13.6 us (25%)
  local copies, waits for them, and re-layouts  5.16 us (9%)
  other arithmetic  4.35 us (8%)
    pallas_call x1, Pallas kernels, gather(): pl.pallas_call(functools.partial(gather_kernel, zn, yn), out_shape=jax.Sh...  26.1 us
    pallas_call x1, Pallas kernels, halo(): pl.pallas_call(functools.partial(halo_kernel, n), out_shape=(edge, edge),...  5.76 us
    unnamed x42, local copies, waits for them, and re-layouts  4.8 us
    dot_general x2, matrix products, attend(): jnp.dot(normed, qkv_weight[:, channels:], preferred_element_type=jnp.floa...  4.47 us
    dot_general x2, matrix products, attend(): jnp.dot(attended, proj_weight, preferred_element_type=jnp.float32)  4.15 us
    dot_general x1, matrix products, causal_conv(): jnp.dot(stacked, kernel.reshape(27 * channels, channels), preferred_eleme...  2.97 us
    dot_general x2, matrix products, attend(): jnp.dot(queries, key_part.T, preferred_element_type=jnp.float32)  1.73 us
    convert_element_type x1, other arithmetic, body(): conv_in = jax.nn.silu(rms_scale(padded, norm_gain)).astype(jnp.bfloat16)  1.67 us

profile of v1, /device:TPU:0, one launch (start us, length us, event | category | flops | bytes accessed | tf_op | source)
XLA Modules:
  0.0 55.2 jit_solution(13797024037248962466)
XLA Ops:
  0.0 0.0 copy-start
  0.0 5.8 %shard_map.73 = (bf16[2,120,384]{2,1,0:T(8,128)(2,1)}, bf16[2,120,384]{2,1,0:T(8,128)(2,1)}) custom-call(bf16[2,1,120,384]{3,2,1,0:T(8,128)(2,1)} %x_ref.1), custom_call_target="tpu_custom_call" | custom-call | tf_op jit(solution)/shard_map/pallas_call | solution.py:70
  5.8 1.3 %fusion.35 = f32[2,3,120]{2,0,1:T(2,128)S(1)} fusion(bf16[2,1,120,384]{3,2,0,1:T(8,128)(2,1)} %bitcast.73, bf16[2,1,120,384]{3,2,0,1:T(8,128)(2,1)} %bitcast.67, bf16[2,1,120,384]{3,2,0,1:T(8,128)(2,1)} %bitcast.71), kind=kLoop, calls=%fused_computation.41 | loop fusion | flops 1381680 | bytes 555840 | tf_op jit(solution)/shard_map/reduce_sum | solution.py:250
  7.1 0.0 slice-start
  7.1 1.7 %fusion.42 = bf16[2,3,120,384]{3,2,0,1:T(8,128)(2,1)S(1)} fusion(f32[384]{0:T(512)} %param.9, f32[2,3,120]{2,0,1:T(2,128)S(1)} %add_rsqrt_fusion, bf16[2,1,120,384]{3,2,0,1:T(8,128)(2,1)} %bitcast.74, bf16[2,1,120,384]{3,2,0,1:T(8,128)(2,1)} %bitcast.68, bf16[2,1,120,384]{3,2,0,1:T(8,128)(2,1)} %bitcast.72), kind=kLoop, calls=%fused_computation.48 | loop fusion | flops 2764800 | bytes 1110336 | tf_op jit(solution)/shard_map/convert_element_type | solution.py:295
  9.2 0.0 copy-start.5
  9.3 0.0 slice-start.1
  9.4 0.1 fusion.70
  9.5 0.1 fusion.71
  9.6 0.1 fusion.72
  9.7 0.1 fusion.73
  9.8 0.1 fusion.74
  9.9 0.1 fusion.75
  9.9 0.2 copy-done.5
  10.1 1.3 %slice-done.1 = s8[3768320]{0:T(1024)(128)(4,1)S(1)} async-done(((s8[7962624]{0:T(1024)(128)(4,1)}), s8[3768320]{0:T(1024)(128)(4,1)S(1)}, s32[]{:S(2)}) %slice-start.1) | async-done | bytes 3768344
  11.4 3.0 %fusion.55 = (f32[2,120]{1,0:T(2,128)S(1)}, bf16[2,1,120,384]{3,2,0,1:T(8,128)(2,1)S(1)}) fusion(bf16[10368,384,1]{1,0,2:T(8,128)(2,1)S(1)} %bitcast.78, bf16[2,1,120,10368]{3,2,0,1:T(8,128)(2,1)S(1)} %fusion.75, bf16[2,1,120,384]{3,2,1,0:T(8,128)(2,1)S(1)} %copy-done.5), kind=kOutput, calls=%fused_computation.64 | convolution fusion | flops 1911582464 | bytes 13308864 | tf_op jit(solution)/shard_map/dot_general | solution.py:265
  14.4 0.1 fusion.60.x_ref
  14.6 0.3 convolution_convert_fusion.2
  14.9 26.1 %shard_map.74 = bf16[2,16,120,384]{3,2,1,0:T(8,128)(2,1)S(1)} custom-call(bf16[2,120,384]{2,1,0:T(8,128)(2,1)S(1)} %fusion.60.x_ref), custom_call_target="tpu_custom_call" | custom-call | tf_op jit(solution)/shard_map/pallas_call | solution.py:229
  40.9 0.3 fusion.76
  41.3 1.7 %convolution_convert_fusion = bf16[1920,768]{1,0:T(8,128)(2,1)S(1)} fusion(bf16[1920,384]{1,0:T(8,128)(2,1)S(1)} %bitcast.70, bf16[384,1152]{1,0:T(8,128)(2,1)S(1)} %copy-done.3), kind=kOutput, calls=%fused_computation.17 | convolution fusion | flops 1133936640 | bytes 5013504 | tf_op jit(solution)/shard_map/dot_general | solution.py:273
  42.9 0.0 copy-start.2
  43.0 1.6 %copy-done.2 = bf16[1920,768]{1,0:T(8,128)(2,1)} copy-done((bf16[1920,768]{1,0:T(8,128)(2,1)}, bf16[1920,768]{1,0:T(8,128)(2,1)S(1)}, u32[]{:S(2)}) %copy-start.2) | copy-done | bytes 2949144
  44.5 0.9 %fusion.77 = (f32[120]{0:T(128)S(1)}, f32[120,1920]{1,0:T(8,128)S(1)}) fusion(bf16[1920,768]{1,0:T(8,128)(2,1)S(1)} %convolution_convert_fusion, bf16[2,120,384]{2,1,0:T(8,128)(2,1)S(1)} %convolution_convert_fusion.2), kind=kOutput, calls=%fused_computation.105 | convolution fusion | flops 177407872 | bytes 2488800 | tf_op jit(solution)/shard_map/dot_general | solution.py:278
  45.4 0.3 fusion.44
  45.7 2.1 %fusion.29 = bf16[1,120,384]{2,1,0:T(8,128)(2,1)S(1)} fusion(bf16[384,384]{1,0:T(8,128)(2,1)S(1)} %copy-done, bf16[1920,768]{1,0:T(8,128)(2,1)} %copy-done.2, f32[120,1920]{1,0:T(8,128)S(1)} %get-tuple-element.14, f32[120]{0:T(128)S(1)} %fusion.44, f32[120]{0:T(128)S(1)} %get-tuple-element.13, bf16[2,1,120,384]{3,2,0,1:T(8,128)(2,1)S(1)} %get-tuple-element.12), kind=kOutput, calls=%fused_computation.39 | convolution fusion | flops 213212160 | bytes 2876352 | tf_op jit(solution)/shard_map/dot_general | solution.py:283
  47.8 2.8 %convolution_convert_fusion.1 = bf16[1920,768]{1,0:T(8,128)(2,1)S(1)} fusion(bf16[1920,384]{1,0:T(8,128)(2,1)S(1)} %bitcast.69, bf16[384,1152]{1,0:T(8,128)(2,1)} %param.12), kind=kOutput, calls=%fused_computation.18 | convolution fusion | flops 1133936640 | bytes 5013504 | tf_op jit(solution)/shard_map/dot_general | solution.py:273
  50.6 0.9 %fusion.78 = (f32[120]{0:T(128)S(1)}, f32[120,1920]{1,0:T(8,128)S(1)}) fusion(bf16[1920,768]{1,0:T(8,128)(2,1)S(1)} %convolution_convert_fusion.1, bf16[2,120,384]{2,1,0:T(8,128)(2,1)S(1)} %convolution_convert_fusion.2), kind=kOutput, calls=%fused_computation.106 | convolution fusion | flops 177407872 | bytes 2488800 | tf_op jit(solution)/shard_map/dot_general | solution.py:278
  51.4 0.7 %copy-done.1 = bf16[1920,768]{1,0:T(8,128)(2,1)} copy-done((bf16[1920,768]{1,0:T(8,128)(2,1)}, bf16[1920,768]{1,0:T(8,128)(2,1)S(1)}, u32[]{:S(2)}) %copy-start.1) | copy-done | bytes 2949144
  52.2 0.3 fusion.43
  52.4 2.1 %fusion.32 = bf16[1,120,384]{2,1,0:T(8,128)(2,1)S(1)} fusion(bf16[384,384]{1,0:T(8,128)(2,1)S(1)} %copy-done, bf16[1920,768]{1,0:T(8,128)(2,1)} %copy-done.1, f32[120,1920]{1,0:T(8,128)S(1)} %get-tuple-element.16, f32[120]{0:T(128)S(1)} %fusion.43, f32[120]{0:T(128)S(1)} %get-tuple-element.15, bf16[2,1,120,384]{3,2,1,0:T(8,128)(2,1)S(1)} %bitcast.75), kind=kOutput, calls=%fused_computation.40 | convolution fusion | flops 213212160 | bytes 2876352 | tf_op jit(solution)/shard_map/dot_general | solution.py:283
  54.5 0.7 %maximum_bitcast_fusion = bf16[2,1,120,384]{3,2,1,0:T(8,128)(2,1)} fusion(bf16[1,120,384]{2,1,0:T(8,128)(2,1)S(1)} %fusion.29, bf16[1,120,384]{2,1,0:T(8,128)(2,1)S(1)} %fusion.32), kind=kLoop, calls=%fused_computation.88 | loop fusion | flops 92160 | bytes 368640 | tf_op jit(solution)/shard_map/reshape | solution.py:310
  (31 shorter events, 0.7 us)
Async XLA Ops:
  0.0 45.7 %copy-start = (bf16[384,384]{1,0:T(8,128)(2,1)S(1)}, bf16[384,384]{1,0:T(8,128)(2,1)}, u32[]{:S(2)}) copy-start(bf16[384,384]{1,0:T(8,128)(2,1)} %param.13) | copy-start | bytes 884740
  7.1 2.9 %slice-start = ((s8[7962624]{0:T(1024)(128)(4,1)}), s8[4194304]{0:T(1024)(128)(4,1)S(1)}, s32[]{:S(2)}) async-start(s8[7962624]{0:T(1024)(128)(4,1)} %bitcast.76), calls=%async_computation | async-start | bytes 8388608
  9.2 0.9 %copy-start.5 = (bf16[2,1,120,384]{3,2,1,0:T(8,128)(2,1)S(1)}, bf16[2,1,120,384]{3,2,1,0:T(8,128)(2,1)}, u32[]{:S(2)}) copy-start(bf16[2,1,120,384]{3,2,1,0:T(8,128)(2,1)} %param.7) | copy-start | bytes 552964
  9.3 2.1 %slice-start.1 = ((s8[7962624]{0:T(1024)(128)(4,1)}), s8[3768320]{0:T(1024)(128)(4,1)S(1)}, s32[]{:S(2)}) async-start(s8[7962624]{0:T(1024)(128)(4,1)} %bitcast.76), calls=%async_computation.1 | async-start | bytes 7536640
  11.4 3.0 %copy-start.4 = (f32[384]{0:T(512)S(1)}, f32[384]{0:T(512)}, u32[]{:S(2)}) copy-start(f32[384]{0:T(512)} %param.11) | copy-start | bytes 4612
  11.4 3.1 %copy-start.3 = (bf16[384,1152]{1,0:T(8,128)(2,1)S(1)}, bf16[384,1152]{1,0:T(8,128)(2,1)}, u32[]{:S(2)}) copy-start(bf16[384,1152]{1,0:T(8,128)(2,1)} %param.12) | copy-start | bytes 2654212
  42.9 1.6 %copy-start.2 = (bf16[1920,768]{1,0:T(8,128)(2,1)}, bf16[1920,768]{1,0:T(8,128)(2,1)S(1)}, u32[]{:S(2)}) copy-start(bf16[1920,768]{1,0:T(8,128)(2,1)S(1)} %convolution_convert_fusion) | copy-start | bytes 8847364
  50.6 1.6 %copy-start.1 = (bf16[1920,768]{1,0:T(8,128)(2,1)}, bf16[1920,768]{1,0:T(8,128)(2,1)S(1)}, u32[]{:S(2)}) copy-start(bf16[1920,768]{1,0:T(8,128)(2,1)S(1)} %convolution_convert_fusion.1) | copy-start | bytes 8847364

commit v2 on v1

--- a/solution.py
+++ b/solution.py
@@ -268,21 +268,27 @@
     return result.reshape(frames, row_count, col_count, channels)
 
 
-def attend(queries, normed, mixed_frame, qkv_weight, proj_weight):
-    channels = queries.shape[-1]
-    key_value = jnp.dot(
-        normed, qkv_weight[:, channels:], preferred_element_type=jnp.float32
-    ).astype(jnp.bfloat16)
-    key_part = key_value[:, :channels]
-    value_part = key_value[:, channels:]
-    scores = jnp.dot(queries, key_part.T, preferred_element_type=jnp.float32) * channels ** (-0.5)
+def halves(values):
+    high = lax.reduce_precision(values, 8, 7)
+    return high.astype(jnp.bfloat16), (values - high).astype(jnp.bfloat16)
+
+
+def dot(a, b):
+    return jnp.dot(a, b, preferred_element_type=jnp.float32)
+
+
+def attend(queries, normed, mixed_frame, value_weight, proj_weight):
+    local, channels = mixed_frame.shape
+    both = lax.dot_general(
+        queries, normed, (((1,), (1,)), ((), ())), preferred_element_type=jnp.float32
+    )
+    scores = (both[:local] + both[local:]) * channels ** (-0.5)
     scores = scores - jnp.max(scores, axis=-1, keepdims=True)
     expo = jnp.exp(scores)
     weights = (expo / jnp.sum(expo, axis=-1, keepdims=True)).astype(jnp.bfloat16)
-    attended = jnp.dot(weights, value_part, preferred_element_type=jnp.float32).astype(jnp.bfloat16)
-    result = mixed_frame.astype(jnp.float32) + jnp.dot(
-        attended, proj_weight, preferred_element_type=jnp.float32
-    )
+    high, low = halves(dot(weights, normed))
+    attended = (dot(high, value_weight) + dot(low, value_weight)).astype(jnp.bfloat16)
+    result = mixed_frame.astype(jnp.float32) + dot(attended, proj_weight)
     return result.astype(jnp.bfloat16)
 
 
@@ -303,9 +309,17 @@
     queries = jnp.dot(
         normed, qkv_weight[:, :channels], preferred_element_type=jnp.float32
     ).astype(jnp.bfloat16)
+    key_weight = qkv_weight[:, channels : 2 * channels]
+    value_weight = qkv_weight[:, 2 * channels :]
+    high, low = halves(
+        lax.dot_general(
+            queries, key_weight, (((2,), (1,)), ((), ())), preferred_element_type=jnp.float32
+        )
+    )
+    queries = jnp.concatenate([high, low], axis=1)
     whole = gather(normed, n).reshape(frames, n * local, channels)
     outs = [
-        attend(queries[f], whole[f], mixed[f], qkv_weight, proj_weight) for f in range(frames)
+        attend(queries[f], whole[f], mixed[f], value_weight, proj_weight) for f in range(frames)
     ]
     return jnp.stack(outs).reshape(block_input.shape)
 

time: 55.5 us -> 47.1 us (0.85)
  matrix products: 13.6 us -> 7.27 us
  local copies, waits for them, and re-layouts: 5.16 us -> 2.85 us
    dot_general x7 -> x9, matrix products: 10.6 us -> 4.29 us  [the longest x6 2.35 us: dot(): return jnp.dot(a, b, preferred_element_type=jnp.float32)]
    unnamed x42 -> x38, local copies, waits for them, and re-layouts: 4.8 us -> 2.49 us
where the time goes in v2:
time: 47.1 us; the launch traced here: 46.9 us
  Pallas kernels  31.8 us (68%)
  matrix products  7.27 us (15%)
  other arithmetic  4.7 us (10%)
  local copies, waits for them, and re-layouts  2.85 us (6%)
    pallas_call x1, Pallas kernels, gather(): pl.pallas_call(functools.partial(gather_kernel, zn, yn), out_shape=jax.Sh...  26.1 us
    pallas_call x1, Pallas kernels, halo(): pl.pallas_call(functools.partial(halo_kernel, n), out_shape=(edge, edge),...  5.76 us
    dot_general x1, matrix products, causal_conv(): jnp.dot(stacked, kernel.reshape(27 * channels, channels), preferred_eleme...  2.99 us
    unnamed x38, local copies, waits for them, and re-layouts  2.49 us
    dot_general x6, matrix products, dot(): return jnp.dot(a, b, preferred_element_type=jnp.float32)  2.35 us
    convert_element_type x1, other arithmetic, body(): conv_in = jax.nn.silu(rms_scale(padded, norm_gain)).astype(jnp.bfloat16)  1.67 us
    dot_general x2, matrix products, attend(): lax.dot_general(queries, normed, (((1,), (1,)), ((), ())), preferred_elem...  1.43 us
    reduce_sum x1, other arithmetic, rms_scale(): jnp.mean(wide * wide, axis=-1, keepdims=True) + 1e-06  1.29 us

profile of v2, /device:TPU:0, one launch (start us, length us, event | category | flops | bytes accessed | tf_op | source)
XLA Modules:
  0.0 46.9 jit_solution(15506842675567161159)
XLA Ops:
  0.0 5.8 %shard_map.73 = (bf16[2,120,384]{2,1,0:T(8,128)(2,1)}, bf16[2,120,384]{2,1,0:T(8,128)(2,1)}) custom-call(bf16[2,1,120,384]{3,2,1,0:T(8,128)(2,1)} %x_ref.1), custom_call_target="tpu_custom_call" | custom-call | tf_op jit(solution)/shard_map/pallas_call | solution.py:70
  5.8 1.3 %fusion.18 = f32[2,3,120]{2,0,1:T(2,128)S(1)} fusion(bf16[2,1,120,384]{3,2,0,1:T(8,128)(2,1)} %bitcast.81, bf16[2,1,120,384]{3,2,0,1:T(8,128)(2,1)} %bitcast.77, bf16[2,1,120,384]{3,2,0,1:T(8,128)(2,1)} %bitcast.79), kind=kLoop, calls=%fused_computation.34 | loop fusion | flops 1381680 | bytes 555840 | tf_op jit(solution)/shard_map/reduce_sum | solution.py:250
  7.1 0.0 slice-start
  7.1 1.7 %fusion.25 = bf16[2,3,120,384]{3,2,0,1:T(8,128)(2,1)S(1)} fusion(f32[384]{0:T(512)} %param.9, f32[2,3,120]{2,0,1:T(2,128)S(1)} %add_rsqrt_fusion, bf16[2,1,120,384]{3,2,0,1:T(8,128)(2,1)} %bitcast.82, bf16[2,1,120,384]{3,2,0,1:T(8,128)(2,1)} %bitcast.78, bf16[2,1,120,384]{3,2,0,1:T(8,128)(2,1)} %bitcast.80), kind=kLoop, calls=%fused_computation.41 | loop fusion | flops 2764800 | bytes 1110336 | tf_op jit(solution)/shard_map/convert_element_type | solution.py:301
  9.2 0.0 copy-start.3
  9.3 0.0 slice-start.1
  9.4 0.1 fusion.66
  9.5 0.1 fusion.67
  9.6 0.1 fusion.68
  9.7 0.1 fusion.69
  9.8 0.1 fusion.70
  9.9 0.1 fusion.71
  9.9 0.2 copy-done.3
  10.1 1.3 %slice-done.1 = s8[3768320]{0:T(1024)(128)(4,1)S(1)} async-done(((s8[7962624]{0:T(1024)(128)(4,1)}), s8[3768320]{0:T(1024)(128)(4,1)S(1)}, s32[]{:S(2)}) %slice-start.1) | async-done | bytes 3768344
  11.4 3.0 %fusion.32 = (f32[2,120]{1,0:T(2,128)S(1)}, bf16[2,1,120,384]{3,2,0,1:T(8,128)(2,1)S(1)}) fusion(bf16[10368,384,1]{1,0,2:T(8,128)(2,1)S(1)} %bitcast.86, bf16[2,1,120,10368]{3,2,0,1:T(8,128)(2,1)S(1)} %fusion.71, bf16[2,1,120,384]{3,2,1,0:T(8,128)(2,1)S(1)} %copy-done.3), kind=kOutput, calls=%fused_computation.59 | convolution fusion | flops 1911582464 | bytes 13308864 | tf_op jit(solution)/shard_map/dot_general | solution.py:265
  14.4 0.1 fusion.56.x_ref
  14.6 0.0 copy-done.1
  14.6 0.5 %reduce-precision_convert_fusion = (bf16[2,120,384]{2,1,0:T(8,128)(2,1)S(1)}, bf16[2,120,384]{2,1,0:T(8,128)(2,1)S(1)}) fusion(bf16[384,1152]{1,0:T(8,128)(2,1)S(1)} %copy-done.1, bf16[2,120,384]{2,1,0:T(8,128)(2,1)S(1)} %fusion.56.x_ref), kind=kOutput, calls=%fused_computation.54 | convolution fusion | flops 142018560 | bytes 1142784 | tf_op jit(solution)/shard_map/dot_general | solution.py:315
  15.1 26.1 %shard_map.74 = bf16[2,16,120,384]{3,2,1,0:T(8,128)(2,1)S(1)} custom-call(bf16[2,120,384]{2,1,0:T(8,128)(2,1)S(1)} %fusion.56.x_ref), custom_call_target="tpu_custom_call" | custom-call | tf_op jit(solution)/shard_map/pallas_call | solution.py:229
  41.2 0.3 fusion.86
  41.5 0.7 %fusion.73 = f32[240,1920]{1,0:T(8,128)S(1)} fusion(bf16[1920,384]{1,0:T(8,128)(2,1)S(1)} %bitcast.73, bf16[2,120,384]{2,1,0:T(8,128)(2,1)S(1)} %get-tuple-element.12, bf16[2,120,384]{2,1,0:T(8,128)(2,1)S(1)} %get-tuple-element.11), kind=kOutput, calls=%fused_computation.102 | convolution fusion | flops 354263040 | bytes 3686400 | tf_op jit(solution)/shard_map/dot_general | solution.py:282
  42.2 0.7 %fusion.54 = f32[240,1920]{1,0:T(8,128)S(1)} fusion(bf16[1920,384]{1,0:T(8,128)(2,1)S(1)} %bitcast.75, bf16[2,120,384]{2,1,0:T(8,128)(2,1)S(1)} %get-tuple-element.11, bf16[2,120,384]{2,1,0:T(8,128)(2,1)S(1)} %get-tuple-element.12), kind=kOutput, calls=%fused_computation.83 | convolution fusion | flops 354263040 | bytes 3686400 | tf_op jit(solution)/shard_map/dot_general | solution.py:282
  42.9 0.3 fusion.83
  43.2 0.3 fusion.28
  43.5 0.5 %fusion.30 = f32[120,384]{1,0:T(8,128)S(1)} fusion(bf16[1920,384]{1,0:T(8,128)(2,1)S(1)} %bitcast.76, f32[120]{0:T(128)S(1)} %fusion.28, f32[120]{0:T(128)S(1)} %get-tuple-element.15, f32[240,1920]{1,0:T(8,128)S(1)} %fusion.54), kind=kOutput, calls=%fused_computation.57 | convolution fusion | flops 178099200 | bytes 3503040 | tf_op jit(solution)/shard_map/dot_general | solution.py:277
  44.1 0.3 fusion.29
  44.4 0.6 %fusion.31 = f32[120,384]{1,0:T(8,128)S(1)} fusion(bf16[1920,384]{1,0:T(8,128)(2,1)S(1)} %bitcast.74, f32[120]{0:T(128)S(1)} %fusion.29, f32[120]{0:T(128)S(1)} %get-tuple-element.16, f32[240,1920]{1,0:T(8,128)S(1)} %fusion.73), kind=kOutput, calls=%fused_computation.58 | convolution fusion | flops 178099200 | bytes 3503040 | tf_op jit(solution)/shard_map/dot_general | solution.py:277
  45.0 0.2 fusion.44
  45.2 0.4 fusion.16
  45.6 0.2 fusion.48
  45.8 0.4 fusion.17
  46.2 0.7 %maximum_bitcast_fusion = bf16[2,1,120,384]{3,2,1,0:T(8,128)(2,1)} fusion(bf16[1,120,384]{2,1,0:T(8,128)(2,1)S(1)} %fusion.16, bf16[1,120,384]{2,1,0:T(8,128)(2,1)S(1)} %fusion.17), kind=kLoop, calls=%fused_computation.107 | loop fusion | flops 92160 | bytes 368640 | tf_op jit(solution)/shard_map/reshape | solution.py:324
  (30 shorter events, 0.7 us)
Async XLA Ops:
  0.0 45.2 %copy-start = (bf16[384,384]{1,0:T(8,128)(2,1)S(1)}, bf16[384,384]{1,0:T(8,128)(2,1)}, u32[]{:S(2)}) copy-start(bf16[384,384]{1,0:T(8,128)(2,1)} %param.13) | copy-start | bytes 884740
  7.1 2.9 %slice-start = ((s8[7962624]{0:T(1024)(128)(4,1)}), s8[4194304]{0:T(1024)(128)(4,1)S(1)}, s32[]{:S(2)}) async-start(s8[7962624]{0:T(1024)(128)(4,1)} %bitcast.84), calls=%async_computation | async-start | bytes 8388608
  9.2 0.9 %copy-start.3 = (bf16[2,1,120,384]{3,2,1,0:T(8,128)(2,1)S(1)}, bf16[2,1,120,384]{3,2,1,0:T(8,128)(2,1)}, u32[]{:S(2)}) copy-start(bf16[2,1,120,384]{3,2,1,0:T(8,128)(2,1)} %param.7) | copy-start | bytes 552964
  9.3 2.1 %slice-start.1 = ((s8[7962624]{0:T(1024)(128)(4,1)}), s8[3768320]{0:T(1024)(128)(4,1)S(1)}, s32[]{:S(2)}) async-start(s8[7962624]{0:T(1024)(128)(4,1)} %bitcast.84), calls=%async_computation.1 | async-start | bytes 7536640
  11.4 3.0 %copy-start.2 = (f32[384]{0:T(512)S(1)}, f32[384]{0:T(512)}, u32[]{:S(2)}) copy-start(f32[384]{0:T(512)} %param.11) | copy-start | bytes 4612
  11.4 3.1 %copy-start.1 = (bf16[384,1152]{1,0:T(8,128)(2,1)S(1)}, bf16[384,1152]{1,0:T(8,128)(2,1)}, u32[]{:S(2)}) copy-start(bf16[384,1152]{1,0:T(8,128)(2,1)} %param.12) | copy-start | bytes 2654212

commit v3 on v2

--- a/solution.py
+++ b/solution.py
@@ -10,7 +10,9 @@
 CORES = 2
 
 
-def halo_kernel(n, x_ref, before_ref, after_ref, sems, recv):
+def halo_kernel(n, x_ref, weight_ref, before_ref, after_ref, held_ref, sems, recv, weight_sem):
+    weight_copy = pltpu.make_async_copy(weight_ref, held_ref, weight_sem)
+    weight_copy.start()
     me = lax.axis_index("tm")
     rows = x_ref.shape[1]
     barrier = pltpu.get_barrier_semaphore()
@@ -62,23 +64,30 @@
         to_previous().wait_send()
         to_next().wait_recv()
 
-
-def halo(x, n):
+    weight_copy.wait()
+
+
+def halo(x, weight, n):
     frames, _, cols, channels = x.shape
     edge = jax.ShapeDtypeStruct((frames, cols, channels), x.dtype)
     vmem = pl.BlockSpec(memory_space=pltpu.VMEM)
     return pl.pallas_call(
         functools.partial(halo_kernel, n),
-        out_shape=(edge, edge),
-        in_specs=[vmem],
-        out_specs=(vmem, vmem),
-        scratch_shapes=[pltpu.SemaphoreType.DMA((2,)), pltpu.SemaphoreType.DMA((2,))],
-        compiler_params=pltpu.CompilerParams(collective_id=0, has_side_effects=True),
-    )(x)
+        out_shape=(edge, edge, jax.ShapeDtypeStruct(weight.shape, weight.dtype)),
+        in_specs=[pl.BlockSpec(memory_space=pltpu.HBM)] * 2,
+        out_specs=(vmem, vmem, vmem),
+        scratch_shapes=[
+            pltpu.SemaphoreType.DMA((2,)),
+            pltpu.SemaphoreType.DMA((2,)),
+            pltpu.SemaphoreType.DMA,
+        ],
+        compiler_params=pltpu.CompilerParams(collective_id=0, has_side_effects=True, vmem_limit_bytes=weight.size * 2 + 4 * 2**20),
+    )(x, weight)
 
 
 def gather_kernel(zn, yn, x_ref, out_ref, local_sem, up, down, across, twin, recv):
-    frames = x_ref.shape[0]
+    splits = x_ref.shape[1]
+    pieces = x_ref.shape[0] * splits
     me = lax.axis_index("tm")
     c = lax.rem(me, CORES)
     y = lax.rem(me // CORES, yn)
@@ -107,11 +116,14 @@
     inner = jnp.logical_and(has_below, has_above)
     pl.semaphore_wait(barrier, yn + (jnp.where(inner, 2, 1) if zn > 1 else 0))
 
+    def landing(owner, f):
+        return out_ref.at[f // splits, owner, f % splits]
+
     def copy(zz, yy, cc, f, send, target, own=False):
         owner = index(zz, yy, cc)
         return pltpu.make_async_remote_copy(
-            x_ref.at[f] if own else out_ref.at[f, owner],
-            out_ref.at[f, owner],
+            x_ref.at[f // splits, f % splits] if own else landing(owner, f),
+            landing(owner, f),
             send,
             recv.at[owner, f],
             device_id={"tm": target},
@@ -133,9 +145,11 @@
         copy(zz, yy, cc, f, up.at[0, 0], sibling).wait_recv()
 
     def own_copy(f):
-        return pltpu.make_async_copy(x_ref.at[f], out_ref.at[f, me], local_sem.at[f])
-
-    for f in range(frames):
+        return pltpu.make_async_copy(
+            x_ref.at[f // splits, f % splits], landing(me, f), local_sem.at[f]
+        )
+
+    for f in range(pieces):
 
         @pl.when(has_above)
         def _():
@@ -155,7 +169,7 @@
         twin_copy(zz, yn - 1 - y, f).start()
 
     def step(d, part):
-        for f in range(frames):
+        for f in range(pieces):
 
             @pl.when(z - d >= 0)
             def _():
@@ -189,19 +203,19 @@
         step(d, along)
         if yn > 1:
             if d == 1:
-                for f in range(frames):
+                for f in range(pieces):
                     from_across(z, f)
             else:
                 step(d - 1, crossed)
     if yn > 1:
         if zn == 1:
-            for f in range(frames):
+            for f in range(pieces):
                 from_across(z, f)
         else:
             step(zn - 1, crossed)
 
     for zz in range(zn):
-        for f in range(frames):
+        for f in range(pieces):
             for yy in range(yn):
                 arrived(zz, yy, 1 - c, f)
                 twin_copy(zz, yy, f).wait_send()
@@ -216,7 +230,7 @@
             def _():
                 down_copy(zz, f).wait_send()
 
-    for f in range(frames):
+    for f in range(pieces):
         own_copy(f).wait()
 
 
@@ -224,23 +238,26 @@
     frames, rows, channels = x.shape
     yn = 2 if n % (2 * CORES) == 0 else 1
     zn = n // (CORES * yn)
+    splits = 3 if rows % 24 == 0 else 1
+    pieces = frames * splits
+    x = x.reshape(frames, splits, rows // splits, channels)
     vmem = pl.BlockSpec(memory_space=pltpu.VMEM)
     dma = pltpu.SemaphoreType.DMA
     return pl.pallas_call(
         functools.partial(gather_kernel, zn, yn),
-        out_shape=jax.ShapeDtypeStruct((frames, n, rows, channels), x.dtype),
+        out_shape=jax.ShapeDtypeStruct((frames, n, *x.shape[1:]), x.dtype),
         in_specs=[vmem],
         out_specs=vmem,
         scratch_shapes=[
-            dma((frames,)),
-            dma((zn, frames)),
-            dma((zn, frames)),
-            dma((zn, frames)),
-            dma((zn, yn, frames)),
-            dma((n, frames)),
+            dma((pieces,)),
+            dma((zn, pieces)),
+            dma((zn, pieces)),
+            dma((zn, pieces)),
+            dma((zn, yn, pieces)),
+            dma((n, pieces)),
         ],
         compiler_params=pltpu.CompilerParams(
-            collective_id=1, has_side_effects=True, vmem_limit_bytes=48 * 2**20
+            collective_id=1, has_side_effects=True, vmem_limit_bytes=(n + 2) * 2 * x.size * 2 + 2**20
         ),
     )(x)
 
@@ -263,7 +280,7 @@
     ]
     stacked = jnp.concatenate(pieces, axis=-1).reshape(-1, 27 * channels)
     result = jnp.dot(
-        stacked, kernel.reshape(27 * channels, channels), preferred_element_type=jnp.float32
+        stacked, kernel, preferred_element_type=jnp.float32
     )
     return result.reshape(frames, row_count, col_count, channels)
 
@@ -296,7 +313,9 @@
     n = lax.axis_size("tm")
     me = lax.axis_index("tm")
     frames, rows, cols, channels = block_input.shape
-    before, after = halo(hidden_state, n)
+    before, after, conv_weight = halo(
+        hidden_state, conv_weight.reshape(-1, conv_weight.shape[-1]), n
+    )
     padded = jnp.concatenate([before[:, None], hidden_state, after[:, None]], axis=1)
     conv_in = jax.nn.silu(rms_scale(padded, norm_gain)).astype(jnp.bfloat16)
     padded = jnp.pad(conv_in, ((2, 0), (0, 0), (1, 1), (0, 0)))

time: 47.1 us -> 46.4 us (0.985)
  local copies, waits for them, and re-layouts: 2.85 us -> 5.72 us
  other arithmetic: 4.7 us -> 2.35 us
  Pallas kernels: 31.8 us -> 30.7 us
    unnamed x38 -> x42, local copies, waits for them, and re-layouts: 2.49 us -> 5.36 us
    convert_element_type x1, other arithmetic: 1.67 us -> 0.41 us  [body(): conv_in = jax.nn.silu(rms_scale(padded, norm_gain)).astype(jnp.bfloat16)]
    reduce_sum x1, other arithmetic: 1.29 us -> 0.19 us  [rms_scale(): jnp.mean(wide * wide, axis=-1, keepdims=True) + 1e-06]
    pallas_call x1, Pallas kernels: 5.76 us -> 4.75 us  [halo(): pl.pallas_call(functools.partial(halo_kernel, n), out_shape=(edge, edge,...]
where the time goes in v3:
time: 46.4 us; the launch traced here: 46.2 us
  Pallas kernels  30.7 us (66%)
  matrix products  7.16 us (15%)
  local copies, waits for them, and re-layouts  5.72 us (12%)
  other arithmetic  2.35 us (5%)
    pallas_call x1, Pallas kernels, gather(): pl.pallas_call(functools.partial(gather_kernel, zn, yn), out_shape=jax.Sh...  26 us
    unnamed x42, local copies, waits for them, and re-layouts  5.36 us
    pallas_call x1, Pallas kernels, halo(): pl.pallas_call(functools.partial(halo_kernel, n), out_shape=(edge, edge,...  4.75 us
    dot_general x1, matrix products, causal_conv(): result = jnp.dot(stacked, kernel, preferred_element_type=jnp.float32)  2.87 us
    dot_general x6, matrix products, dot(): return jnp.dot(a, b, preferred_element_type=jnp.float32)  2.36 us
    dot_general x2, matrix products, attend(): lax.dot_general(queries, normed, (((1,), (1,)), ((), ())), preferred_elem...  1.43 us

profile of v3, /device:TPU:0, one launch (start us, length us, event | category | flops | bytes accessed | tf_op | source)
XLA Modules:
  0.0 46.2 jit_solution(8696011388547714542)
XLA Ops:
  0.1 0.0 copy-start.5
  0.3 0.0 copy-start.1
  0.3 3.3 %copy-done.1 = bf16[3,3,3,384,384]{4,3,2,1,0:T(8,128)(2,1)S(1)} copy-done((bf16[3,3,3,384,384]{4,3,2,1,0:T(8,128)(2,1)S(1)}, bf16[3,3,3,384,384]{4,3,2,1,0:T(8,128)(2,1)}, u32[]{:S(2)}) %copy-start.1) | copy-done | bytes 7962648
  3.6 0.9 %copy-done.2 = bf16[2,1,120,384]{3,2,1,0:T(8,128)(2,1)S(1)} copy-done((bf16[2,1,120,384]{3,2,1,0:T(8,128)(2,1)S(1)}, bf16[2,1,120,384]{3,2,1,0:T(8,128)(2,1)}, u32[]{:S(2)}) %copy-start.2) | copy-done | bytes 184344
  4.5 4.7 %shard_map.73 = (bf16[2,120,384]{2,1,0:T(8,128)(2,1)S(1)}, bf16[2,120,384]{2,1,0:T(8,128)(2,1)S(1)}, bf16[10368,384]{1,0:T(8,128)(2,1)S(1)}) custom-call(bf16[2,1,120,384]{3,2,1,0:T(8,128)(2,1)S(1)} %copy-done.2, bf16[10368,384]{1,0:T(8,128)(2,1)S(1)} %bitcast.85), custom_call_target="tpu_custom_call" | custom-call | tf_op jit(solution)/shard_map/pallas_call | solution.py:74
  9.3 0.2 fusion.25
  9.5 0.4 fusion.32
  10.0 0.0 copy-start.7
  10.3 0.1 fusion.72
  10.4 0.1 fusion.73
  10.4 0.1 fusion.74
  10.5 0.1 fusion.75
  10.6 0.1 fusion.76
  10.7 0.1 fusion.77
  10.7 0.2 copy-done.7
  10.9 2.9 %fusion.39 = (f32[2,120]{1,0:T(2,128)S(1)}, bf16[2,1,120,384]{3,2,0,1:T(8,128)(2,1)S(1)}) fusion(bf16[10368,384]{1,0:T(8,128)(2,1)S(1)} %get-tuple-element.10, bf16[2,1,120,10368]{3,2,0,1:T(8,128)(2,1)S(1)} %fusion.77, bf16[2,1,120,384]{3,2,1,0:T(8,128)(2,1)S(1)} %copy-done.7), kind=kOutput, calls=%fused_computation.60 | convolution fusion | flops 1911582464 | bytes 13308864 | tf_op jit(solution)/shard_map/dot_general | solution.py:282
  13.8 0.1 fusion.41
  14.0 0.5 %reduce-precision_convert_fusion = (bf16[2,120,384]{2,1,0:T(8,128)(2,1)S(1)}, bf16[2,120,384]{2,1,0:T(8,128)(2,1)S(1)}) fusion(bf16[384,1152]{1,0:T(8,128)(2,1)S(1)} %copy-done.4, bf16[2,1,120,384]{3,2,0,1:T(8,128)(2,1)S(1)} %fusion.41), kind=kOutput, calls=%fused_computation.55 | convolution fusion | flops 142018560 | bytes 1142784 | tf_op jit(solution)/shard_map/dot_general | solution.py:334
  14.5 26.0 %shard_map.74 = bf16[2,16,3,40,384]{4,3,2,1,0:T(8,128)(2,1)S(1)} custom-call(bf16[2,3,40,384]{3,2,1,0:T(8,128)(2,1)S(1)} %bitcast.92), custom_call_target="tpu_custom_call" | custom-call | tf_op jit(solution)/shard_map/pallas_call | solution.py:246
  40.4 0.3 fusion.94
  40.8 0.7 %fusion.79 = f32[240,1920]{1,0:T(8,128)S(1)} fusion(bf16[1920,384]{1,0:T(8,128)(2,1)S(1)} %bitcast.93, bf16[2,120,384]{2,1,0:T(8,128)(2,1)S(1)} %get-tuple-element.14, bf16[2,120,384]{2,1,0:T(8,128)(2,1)S(1)} %get-tuple-element.13), kind=kOutput, calls=%fused_computation.102 | convolution fusion | flops 354263040 | bytes 3686400 | tf_op jit(solution)/shard_map/dot_general | solution.py:299
  41.5 0.7 %fusion.61 = f32[240,1920]{1,0:T(8,128)S(1)} fusion(bf16[1920,384]{1,0:T(8,128)(2,1)S(1)} %bitcast.95, bf16[2,120,384]{2,1,0:T(8,128)(2,1)S(1)} %get-tuple-element.13, bf16[2,120,384]{2,1,0:T(8,128)(2,1)S(1)} %get-tuple-element.14), kind=kOutput, calls=%fused_computation.84 | convolution fusion | flops 354263040 | bytes 3686400 | tf_op jit(solution)/shard_map/dot_general | solution.py:299
  42.2 0.3 fusion.91
  42.5 0.3 fusion.35
  42.8 0.5 %fusion.37 = f32[120,384]{1,0:T(8,128)S(1)} fusion(bf16[1920,384]{1,0:T(8,128)(2,1)S(1)} %bitcast.96, f32[120]{0:T(128)S(1)} %fusion.35, f32[120]{0:T(128)S(1)} %get-tuple-element.17, f32[240,1920]{1,0:T(8,128)S(1)} %fusion.61), kind=kOutput, calls=%fused_computation.58 | convolution fusion | flops 178099200 | bytes 3503040 | tf_op jit(solution)/shard_map/dot_general | solution.py:294
  43.4 0.3 fusion.36
  43.7 0.6 %fusion.38 = f32[120,384]{1,0:T(8,128)S(1)} fusion(bf16[1920,384]{1,0:T(8,128)(2,1)S(1)} %bitcast.94, f32[120]{0:T(128)S(1)} %fusion.36, f32[120]{0:T(128)S(1)} %get-tuple-element.18, f32[240,1920]{1,0:T(8,128)S(1)} %fusion.79), kind=kOutput, calls=%fused_computation.59 | convolution fusion | flops 178099200 | bytes 3503040 | tf_op jit(solution)/shard_map/dot_general | solution.py:294
  44.2 0.2 fusion.51
  44.5 0.4 fusion.23
  44.9 0.2 fusion.55
  45.1 0.4 fusion.24
  45.5 0.7 %maximum_bitcast_fusion = bf16[2,1,120,384]{3,2,1,0:T(8,128)(2,1)} fusion(bf16[1,120,384]{2,1,0:T(8,128)(2,1)S(1)} %fusion.23, bf16[1,120,384]{2,1,0:T(8,128)(2,1)S(1)} %fusion.24), kind=kLoop, calls=%fused_computation.107 | loop fusion | flops 92160 | bytes 368640 | tf_op jit(solution)/shard_map/reshape | solution.py:343
  (33 shorter events, 0.7 us)
Async XLA Ops:
  0.0 44.5 %copy-start = (bf16[384,384]{1,0:T(8,128)(2,1)S(1)}, bf16[384,384]{1,0:T(8,128)(2,1)}, u32[]{:S(2)}) copy-start(bf16[384,384]{1,0:T(8,128)(2,1)} %param.13) | copy-start | bytes 884740
  0.0 9.3 %copy-start.3 = (bf16[2,1,120,384]{3,2,1,0:T(8,128)(2,1)S(1)}, bf16[2,1,120,384]{3,2,1,0:T(8,128)(2,1)}, u32[]{:S(2)}) copy-start(bf16[2,1,120,384]{3,2,1,0:T(8,128)(2,1)} %x_ref.1) | copy-start | bytes 552964
  0.1 9.4 %copy-start.5 = (f32[384]{0:T(512)S(1)}, f32[384]{0:T(512)}, u32[]{:S(2)}) copy-start(f32[384]{0:T(512)} %param.9) | copy-start | bytes 4612
  0.3 3.3 %copy-start.1 = (bf16[3,3,3,384,384]{4,3,2,1,0:T(8,128)(2,1)S(1)}, bf16[3,3,3,384,384]{4,3,2,1,0:T(8,128)(2,1)}, u32[]{:S(2)}) copy-start(bf16[3,3,3,384,384]{4,3,2,1,0:T(8,128)(2,1)} %param.10) | copy-start | bytes 23887876
  3.6 0.9 %copy-start.2 = (bf16[2,1,120,384]{3,2,1,0:T(8,128)(2,1)S(1)}, bf16[2,1,120,384]{3,2,1,0:T(8,128)(2,1)}, u32[]{:S(2)}) copy-start(bf16[2,1,120,384]{3,2,1,0:T(8,128)(2,1)} %x_ref.1) | copy-start | bytes 552964
  10.0 0.9 %copy-start.7 = (bf16[2,1,120,384]{3,2,1,0:T(8,128)(2,1)S(1)}, bf16[2,1,120,384]{3,2,1,0:T(8,128)(2,1)}, u32[]{:S(2)}) copy-start(bf16[2,1,120,384]{3,2,1,0:T(8,128)(2,1)} %param.7) | copy-start | bytes 552964
  10.9 2.9 %copy-start.6 = (f32[384]{0:T(512)S(1)}, f32[384]{0:T(512)}, u32[]{:S(2)}) copy-start(f32[384]{0:T(512)} %param.11) | copy-start | bytes 4612
  10.9 3.0 %copy-start.4 = (bf16[384,1152]{1,0:T(8,128)(2,1)S(1)}, bf16[384,1152]{1,0:T(8,128)(2,1)}, u32[]{:S(2)}) copy-start(bf16[384,1152]{1,0:T(8,128)(2,1)} %param.12) | copy-start | bytes 2654212
